TPU v7x, 32 devices: a whole 2x2x4 slice. The times are simulated.
32 devices in a mesh: rows: 8 (over y, x, core), cols: 4 (over z).
Axes of the slice: x: 2, y: 2, z: 4, core: 2. Of those that a mesh axis runs over, the one named last changes fastest.
Arguments:
- white_real: float32 [4096, 4096], P('rows', 'cols'), may hold values from -6 to 6
- white_imag: float32 [4096, 4096], P('rows', 'cols'), may hold values from -6 to 6
- covariates: bfloat16 [16, 4096, 4096], P(None, 'rows', 'cols'), may hold values from -6 to 6
- coefficients: float32 [16], replicated, may hold values from -0.9 to 0.9
- counts: int32 [4096, 4096], P('rows', 'cols'), may hold values from 0 to 5
- land_mask: int32 [4096, 4096], P('rows', 'cols'), may hold values from 0 to 1
- field_hyper: float32 [2], replicated, may hold values from 1 to 2
Outputs:
- step_real: float32 [4096, 4096], P('rows', 'cols')
- step_imag: float32 [4096, 4096], P('rows', 'cols')
- coef_grad: float32 [16], replicated
- objective: float32 [], replicated
All inputs are finite; a program needn't handle non-finite values.
Results may differ from a plain program's by a relative error of at most 0.0003.
Values sent between devices are 32-bit elements; how exact they have to be, the bound alone decides.
No kernel may reach another device: no remote copies, remote signals or barrier semaphores. Data moves between devices by JAX's collectives and lax.ppermute only.
A program may use at most 128 MiB of HBM per device.

v0:
```python
import math
import jax
import jax.numpy as jnp
from jax import lax
from jax.sharding import PartitionSpec as P

NG = 4096
lasso_weight = 0.02
ridge_weight = 0.1


def field_spectrum(field_hyper, wave_row, wave_col):
    amplitude = 0.2 * field_hyper[0]
    freq_range = field_hyper[1]
    radius = (wave_row[:, None] * wave_row[:, None] + wave_col[None, :] * wave_col[None, :]) / (
        freq_range * freq_range
    )
    return amplitude * (1.0 + NG / freq_range * jnp.power(1.0 + radius, -0.75))


def angle_table(left_len, right_len, modulus):
    product = lax.iota(jnp.int32, left_len)[:, None] * lax.iota(jnp.int32, right_len)[None, :]
    angles = (product % modulus).astype(jnp.float32) * (2.0 * math.pi / modulus)
    return (jnp.cos(angles), jnp.sin(angles))


def inverse_transform(pieces, want_real):
    highest = lax.Precision.HIGHEST
    components = pieces.shape[0]
    row_count = pieces.shape[1]
    length = pieces.shape[2]
    factor = 8
    others = length // factor
    shaped = pieces.reshape(components, row_count, others, factor)
    big_cos, big_sin = angle_table(others, others, others)

    def apply_big(table, block):
        return jnp.einsum("rnm,nk->rmk", block, table, precision=highest)

    if components == 2:
        real_mid = apply_big(big_cos, shaped[0]) - apply_big(big_sin, shaped[1])
        imag_mid = apply_big(big_sin, shaped[0]) + apply_big(big_cos, shaped[1])
    else:
        real_mid = apply_big(big_cos, shaped[0])
        imag_mid = apply_big(big_sin, shaped[0])
    tw_cos, tw_sin = angle_table(factor, others, length)
    real_tw = real_mid * tw_cos - imag_mid * tw_sin
    imag_tw = real_mid * tw_sin + imag_mid * tw_cos
    small_cos, small_sin = angle_table(factor, factor, factor)

    def apply_small(table, block):
        return jnp.einsum("rmk,mj->rjk", block, table, precision=highest)

    real_out = (apply_small(small_cos, real_tw) - apply_small(small_sin, imag_tw)).reshape(
        1, row_count, length
    )
    if want_real:
        return real_out
    imag_out = (apply_small(small_sin, real_tw) + apply_small(small_cos, imag_tw)).reshape(
        1, row_count, length
    )
    return jnp.concatenate([real_out, imag_out], axis=0)


def middle_step(spread):
    returned = lax.all_to_all(spread, "cols", split_axis=2, concat_axis=1, tiled=True)
    flipped = jnp.swapaxes(returned, 1, 2)
    return lax.all_to_all(flipped, "rows", split_axis=1, concat_axis=2, tiled=True)


def grid_transform(pieces, want_real):
    full_rows = lax.all_to_all(pieces, "cols", split_axis=1, concat_axis=2, tiled=True)
    halfway = inverse_transform(full_rows, False)
    columns = middle_step(halfway)
    second = inverse_transform(columns, want_real)
    blocks_out = lax.all_to_all(second, "rows", split_axis=2, concat_axis=1, tiled=True)
    return jnp.swapaxes(blocks_out, 1, 2) * (1.0 / NG)


def shards(white_real, white_imag, covariates, coefficients, counts, land_mask, field_hyper):
    highest = lax.Precision.HIGHEST
    rows_here = white_real.shape[0]
    cols_here = white_real.shape[1]
    freq_row = lax.axis_index("rows") * rows_here + lax.iota(jnp.int32, rows_here)
    freq_col = lax.axis_index("cols") * cols_here + lax.iota(jnp.int32, cols_here)
    wave_row = jnp.minimum(freq_row, NG - freq_row).astype(jnp.float32)
    wave_col = jnp.minimum(freq_col, NG - freq_col).astype(jnp.float32)
    spectrum = field_spectrum(field_hyper, wave_row, wave_col)
    scaled = jnp.stack([spectrum * white_real, spectrum * white_imag])
    latent = grid_transform(scaled, True)[0]
    cov_full = covariates.astype(jnp.float32)
    linear = jnp.einsum("j,jrc->rc", coefficients, cov_full, precision=highest)
    log_rate = linear + latent
    intensity = jnp.exp(log_rate)
    land_vals = land_mask.astype(jnp.float32)
    count_vals = counts.astype(jnp.float32)
    residual = land_vals * (intensity - count_vals)
    partial_coef = jnp.einsum("jrc,rc->j", cov_full, residual, precision=highest)
    partial_loss = jnp.sum(land_vals * (intensity - count_vals * log_rate)) + 0.5 * jnp.sum(
        white_real * white_real + white_imag * white_imag
    )
    adjoint = grid_transform(residual[None], False)
    total_coef, total_loss = lax.psum((partial_coef, partial_loss), ("rows", "cols"))
    per_cell = 1.0 / (NG * NG)
    coef_grad = (
        total_coef * per_cell + lasso_weight * jnp.sign(coefficients) + ridge_weight * coefficients
    )
    objective = (
        total_loss * per_cell
        + lasso_weight * jnp.sum(jnp.abs(coefficients))
        + 0.5 * ridge_weight * jnp.sum(coefficients * coefficients)
    )
    curvature = 1.0 + spectrum * spectrum
    step_real = (spectrum * adjoint[0] + white_real) / curvature
    step_imag = (white_imag - spectrum * adjoint[1]) / curvature
    return (step_real, step_imag, coef_grad, objective)


def solution(mesh):
    return jax.shard_map(
        shards,
        mesh=mesh,
        in_specs=(
            P("rows", "cols"),
            P("rows", "cols"),
            P(None, "rows", "cols"),
            P(),
            P("rows", "cols"),
            P("rows", "cols"),
            P(),
        ),
        out_specs=(P("rows", "cols"), P("rows", "cols"), P(), P()),
        check_vma=False,
    )
```

profile of v0, /device:TPU:0, one launch (start us, length us, event | category | flops | bytes accessed | tf_op | source)
XLA Modules:
  0.0 896.9 jit_solution(2084490301962304620)
XLA Ops:
  4.6 3.8 multiply_bitcast_fusion
  12.1 5.8 pad_maximum_fusion
  17.9 6.5 all-to-all-start
  24.5 93.3 %all-to-all-done = f32[2,512,1024]{2,0,1:T(2,128)} async-done(((f32[2,512,1024]{2,0,1:T(2,128)}), f32[2,512,1024]{2,0,1:T(2,128)}, u32[]{:S(2)}, u32[]{:S(2)}) %all-to-all-start) | async-done | bytes 4194336 | tf_op jit(solution)/shard_map/all_to_all | solution.py:72
  117.8 3.5 copy.149
  127.4 10.3 %fusion.62 = f32[128,8,512]{2,0,1:T(8,128)} fusion(f32[128,512,8]{1,0,2:T(8,128)} %copy.151), kind=kOutput, calls=%fused_computation.88 | convolution fusion | flops 3224895488 | bytes 4194304 | tf_op jit(solution)/shard_map/rnm,nk->rmk/dot_general | solution.py:38
  137.6 8.4 fusion.74
  149.8 9.9 %convolution_subtract_fusion.2 = f32[128,8,512]{2,0,1:T(8,128)S(1)} fusion(f32[128,8,512]{2,0,1:T(8,128)} %fusion.74, f32[128,512,8]{1,0,2:T(8,128)S(1)} %copy.153), kind=kOutput, calls=%fused_computation.73 | convolution fusion | flops 3225419776 | bytes 6291456 | tf_op jit(solution)/shard_map/rnm,nk->rmk/dot_general | solution.py:38
  159.8 9.2 %multiply_subtract_fusion.3 = (f32[128,8,512]{2,0,1:T(8,128)S(1)}, f32[128,8,512]{2,0,1:T(8,128)S(1)}) fusion(f32[128,8,512]{2,0,1:T(8,128)S(1)} %convolution_subtract_fusion.2, f32[8,512]{1,0:T(8,128)S(1)} %get-tuple-element.32, f32[8,512]{1,0:T(8,128)S(1)} %get-tuple-element.33, f32[128,8,512]{2,0,1:T(8,128)S(1)} %copy-done.8, f32[128,512,8]{1,0,2:T(8,128)S(1)} %copy.153), kind=kOutput, calls=%fused_computation.41 | convolution fusion | flops 3228565504 | bytes 10518528 | tf_op jit(solution)/shard_map/rnm,nk->rmk/dot_general | solution.py:38
  177.6 4.3 add_bitcast_fusion.2
  186.9 5.3 pad_maximum_fusion.1
  192.2 95.3 %all_to_all.114 = f32[2,128,4096]{1,0,2:T(2,128)S(1)} all-to-all(f32[2,128,4096]{1,0,2:T(2,128)S(1)} %pad_maximum_fusion.1), channel_id=1, replica_groups=mesh['rows'=8,'cols'=4] {'cols'}, dimensions={2} | all-to-all | bytes 8388608 | tf_op jit(solution)/shard_map/all_to_all | solution.py:66
  289.8 5.4 copy.163
  295.2 7.3 copy.164
  302.5 52.9 %all_to_all.115 = f32[2,1024,512]{2,0,1:T(2,128)S(1)} all-to-all(f32[2,1024,512]{2,0,1:T(2,128)} %copy.164), channel_id=1, replica_groups=mesh['rows'=8,'cols'=4] {'rows'}, dimensions={1} | all-to-all | bytes 8388608 | tf_op jit(solution)/shard_map/all_to_all | solution.py:68
  362.6 10.3 %fusion.59 = f32[128,8,512]{2,0,1:T(8,128)} fusion(f32[128,512,8]{1,0,2:T(8,128)} %copy.167), kind=kOutput, calls=%fused_computation.85 | convolution fusion | flops 3224895488 | bytes 4194304 | tf_op jit(solution)/shard_map/rnm,nk->rmk/dot_general | solution.py:38
  372.9 8.4 fusion.71
  385.0 9.9 %convolution_subtract_fusion.1 = f32[128,8,512]{2,0,1:T(8,128)S(1)} fusion(f32[128,8,512]{2,0,1:T(8,128)} %fusion.71, f32[128,512,8]{1,0,2:T(8,128)S(1)} %copy.169), kind=kOutput, calls=%fused_computation.71 | convolution fusion | flops 3225419776 | bytes 6291456 | tf_op jit(solution)/shard_map/rnm,nk->rmk/dot_general | solution.py:38
  395.0 9.2 %multiply_subtract_fusion.2 = (f32[128,8,512]{2,0,1:T(8,128)S(1)}, f32[128,8,512]{2,0,1:T(8,128)S(1)}) fusion(f32[128,8,512]{2,0,1:T(8,128)S(1)} %convolution_subtract_fusion.1, f32[8,512]{1,0:T(8,128)S(1)} %get-tuple-element.32, f32[8,512]{1,0:T(8,128)S(1)} %get-tuple-element.33, f32[128,8,512]{2,0,1:T(8,128)S(1)} %copy-done.9, f32[128,512,8]{1,0,2:T(8,128)S(1)} %copy.169), kind=kOutput, calls=%fused_computation.37 | convolution fusion | flops 3228565504 | bytes 10518528 | tf_op jit(solution)/shard_map/rnm,nk->rmk/dot_general | solution.py:38
  411.8 3.9 all-to-all-start.3
  415.8 22.7 %fusion = f32[1,512,1024]{2,0,1:T(1,128)} fusion(bf16[16,512,1024]{2,1,0:T(8,128)(2,1)} %param.9, f32[16]{0:T(128)S(1)} %copy-done.18), kind=kOutput, calls=%fused_computation.1 | convolution fusion | flops 100663296 | bytes 18874432 | tf_op jit(solution)/shard_map/j,jrc->rc/dot_general | solution.py:92
  438.4 3.9 all-to-all-done.3
  444.5 3.1 multiply_reduce_fusion.1
  449.1 48.1 %all_to_all.116 = f32[1,512,1024]{2,0,1:T(1,128)S(1)} all-to-all(f32[1,512,1024]{2,0,1:T(1,128)S(1)} %broadcast_in_dim.2), channel_id=1, replica_groups=mesh['rows'=8,'cols'=4] {'cols'}, dimensions={1} | all-to-all | bytes 4194304 | tf_op jit(solution)/shard_map/all_to_all | solution.py:72
  501.4 8.4 fusion.68
  509.8 9.0 %multiply_subtract_fusion.1 = (f32[128,8,512]{2,0,1:T(8,128)S(1)}, f32[128,8,512]{2,0,1:T(8,128)S(1)}) fusion(f32[128,8,512]{2,0,1:T(8,128)S(1)} %fusion.68, f32[8,512]{1,0:T(8,128)S(1)} %get-tuple-element.32, f32[8,512]{1,0:T(8,128)S(1)} %get-tuple-element.33, f32[128,512,8]{1,0,2:T(8,128)S(1)} %copy.177), kind=kOutput, calls=%fused_computation.33 | convolution fusion | flops 3228041216 | bytes 8421376 | tf_op jit(solution)/shard_map/rnm,nk->rmk/dot_general | solution.py:38
  527.5 4.3 add_bitcast_fusion.1
  531.7 3.1 copy.213
  536.7 5.3 pad_maximum_fusion.2
  542.0 94.5 %all_to_all.117 = f32[2,128,4096]{1,0,2:T(2,128)S(1)} all-to-all(f32[2,128,4096]{1,0,2:T(2,128)S(1)} %pad_maximum_fusion.2), channel_id=1, replica_groups=mesh['rows'=8,'cols'=4] {'cols'}, dimensions={2} | all-to-all | bytes 8388608 | tf_op jit(solution)/shard_map/all_to_all | solution.py:66
  638.8 5.4 copy.186
  644.2 7.3 copy.187
  651.5 54.8 %all_to_all.118 = f32[2,1024,512]{2,0,1:T(2,128)S(1)} all-to-all(f32[2,1024,512]{2,0,1:T(2,128)} %copy.187), channel_id=1, replica_groups=mesh['rows'=8,'cols'=4] {'rows'}, dimensions={1} | all-to-all | bytes 8388608 | tf_op jit(solution)/shard_map/all_to_all | solution.py:68
  713.5 10.3 %fusion.54 = f32[128,8,512]{2,0,1:T(8,128)} fusion(f32[128,512,8]{1,0,2:T(8,128)} %copy.190), kind=kOutput, calls=%fused_computation.80 | convolution fusion | flops 3224895488 | bytes 4194304 | tf_op jit(solution)/shard_map/rnm,nk->rmk/dot_general | solution.py:38
  723.8 8.4 fusion.66
  736.0 9.9 %convolution_subtract_fusion = f32[128,8,512]{2,0,1:T(8,128)S(1)} fusion(f32[128,8,512]{2,0,1:T(8,128)} %fusion.66, f32[128,512,8]{1,0,2:T(8,128)S(1)} %copy.192), kind=kOutput, calls=%fused_computation.69 | convolution fusion | flops 3225419776 | bytes 6291456 | tf_op jit(solution)/shard_map/rnm,nk->rmk/dot_general | solution.py:38
  745.9 9.2 %multiply_subtract_fusion = (f32[128,8,512]{2,0,1:T(8,128)S(1)}, f32[128,8,512]{2,0,1:T(8,128)S(1)}) fusion(f32[128,8,512]{2,0,1:T(8,128)S(1)} %convolution_subtract_fusion, f32[8,512]{1,0:T(8,128)S(1)} %get-tuple-element.32, f32[8,512]{1,0:T(8,128)S(1)} %get-tuple-element.33, f32[128,8,512]{2,0,1:T(8,128)S(1)} %copy-done.7, f32[128,512,8]{1,0,2:T(8,128)S(1)} %copy.192), kind=kOutput, calls=%fused_computation.29 | convolution fusion | flops 3228565504 | bytes 10518528 | tf_op jit(solution)/shard_map/rnm,nk->rmk/dot_general | solution.py:38
  763.8 4.3 add_bitcast_fusion
  768.1 3.1 copy.215
  773.0 6.8 pad_maximum_fusion.3
  779.8 4.7 all-to-all-start.7
  784.5 7.5 multiply_reduce_fusion
  792.0 41.6 %all-to-all-done.7 = f32[2,128,4096]{1,0,2:T(2,128)} async-done(((f32[2,128,4096]{1,0,2:T(2,128)}), f32[2,128,4096]{1,0,2:T(2,128)}, u32[]{:S(2)}, u32[]{:S(2)}) %all-to-all-start.7) | async-done | bytes 4194336 | tf_op jit(solution)/shard_map/all_to_all | solution.py:76
  833.6 3.9 broadcast_multiply_fusion
  837.6 4.4 copy.274
  842.0 5.0 mul.767
  847.0 6.2 fusion.5
  854.6 38.0 %all-reduce = (f32[16]{0:T(128)S(1)}, f32[]{:T(128)}) all-reduce(f32[16]{0:T(128)S(1)} %multiply_reduce_fusion, f32[]{:T(128)S(6)} %add.265), channel_id=1, replica_groups=mesh['rows'=8,'cols'=4] {'rows','cols'}, use_global_device_ids=true, to_apply=%region_0.1 | all-reduce | flops 17 | bytes 136 | tf_op jit(solution)/shard_map/psum | solution.py:103
  (85 shorter events, 92.7 us)
Async XLA Ops:
  3.9 4.5 copy-start.16
  4.0 4.5 copy-start.14
  17.9 99.9 %all-to-all-start = ((f32[2,512,1024]{2,0,1:T(2,128)}), f32[2,512,1024]{2,0,1:T(2,128)}, u32[]{:S(2)}, u32[]{:S(2)}) async-start(f32[2,512,1024]{2,0,1:T(2,128)} %pad_maximum_fusion), calls=%async_computation | async-start | bytes 8388608 | tf_op jit(solution)/shard_map/all_to_all | solution.py:72
  127.4 10.3 %copy-start.10 = (f32[128,512,8]{1,0,2:T(8,128)S(1)}, f32[128,512,8]{1,0,2:T(8,128)}, u32[]{:S(2)}) copy-start(f32[128,512,8]{1,0,2:T(8,128)} %copy.151) | copy-start | bytes 6291460
  137.6 8.4 copy-start.3
  149.8 10.0 %copy-start.8 = (f32[128,8,512]{2,0,1:T(8,128)S(1)}, f32[128,8,512]{2,0,1:T(8,128)}, u32[]{:S(2)}) copy-start(f32[128,8,512]{2,0,1:T(8,128)} %fusion.62) | copy-start | bytes 6291460
  362.6 10.3 %copy-start.11 = (f32[128,512,8]{1,0,2:T(8,128)S(1)}, f32[128,512,8]{1,0,2:T(8,128)}, u32[]{:S(2)}) copy-start(f32[128,512,8]{1,0,2:T(8,128)} %copy.167) | copy-start | bytes 6291460
  372.9 8.4 copy-start.4
  385.0 10.0 %copy-start.9 = (f32[128,8,512]{2,0,1:T(8,128)S(1)}, f32[128,8,512]{2,0,1:T(8,128)}, u32[]{:S(2)}) copy-start(f32[128,8,512]{2,0,1:T(8,128)} %fusion.59) | copy-start | bytes 6291460
  411.8 3.9 copy-start.18
  411.8 30.5 %all-to-all-start.3 = ((f32[1,128,4096]{1,0,2:T(1,128)}), f32[1,128,4096]{1,0,2:T(1,128)S(1)}, u32[]{:S(2)}, u32[]{:S(2)}) async-start(f32[1,128,4096]{1,0,2:T(1,128)} %bitcast.209), calls=%async_computation.3 | async-start | bytes 4194304 | tf_op jit(solution)/shard_map/all_to_all | solution.py:76
  442.3 2.1 copy-start.6
  442.3 2.2 copy-start.13
  447.6 1.4 copy-start
  713.5 10.3 %copy-start.12 = (f32[128,512,8]{1,0,2:T(8,128)S(1)}, f32[128,512,8]{1,0,2:T(8,128)}, u32[]{:S(2)}) copy-start(f32[128,512,8]{1,0,2:T(8,128)} %copy.190) | copy-start | bytes 6291460
  723.8 8.4 copy-start.5
  736.0 10.0 %copy-start.7 = (f32[128,8,512]{2,0,1:T(8,128)S(1)}, f32[128,8,512]{2,0,1:T(8,128)}, u32[]{:S(2)}) copy-start(f32[128,8,512]{2,0,1:T(8,128)} %fusion.54) | copy-start | bytes 6291460
  779.8 4.7 copy-start.1
  779.8 53.8 %all-to-all-start.7 = ((f32[2,128,4096]{1,0,2:T(2,128)}), f32[2,128,4096]{1,0,2:T(2,128)}, u32[]{:S(2)}, u32[]{:S(2)}) async-start(f32[2,128,4096]{1,0,2:T(2,128)} %pad_maximum_fusion.3), calls=%async_computation.7 | async-start | bytes 8388608 | tf_op jit(solution)/shard_map/all_to_all | solution.py:76
  842.0 5.0 copy-start.2
  842.0 5.0 copy-start.15
  842.0 5.0 copy-start.17
where the time goes:
time: 906 us; the launch traced here: 897 us
  blocking collectives  384 us (42%)
  matrix products  198 us (22%)
  waiting for transfers between devices  139 us (15%)
  local copies, waits for them, and re-layouts  102 us (11%)
  other arithmetic  51.1 us (6%)
  starting transfers between devices  15.1 us (2%)
    all_to_all x2, blocking collectives, middle_step(): lax.all_to_all(spread, 'cols', split_axis=2, concat_axis=1, tiled=True)  190 us
    dot_general x14, matrix products, apply_big(): return jnp.einsum('rnm,nk->rmk', block, table, precision=highest)  131 us
    all_to_all x2, blocking collectives, middle_step(): lax.all_to_all(flipped, 'rows', split_axis=1, concat_axis=2, tiled=True)  108 us
    all_to_all x1, waiting for transfers between devices, grid_transform(): lax.all_to_all(pieces, 'cols', split_axis=1, concat_axis=2, tiled=True)  93.3 us
    all_to_all x1, blocking collectives, grid_transform(): lax.all_to_all(pieces, 'cols', split_axis=1, concat_axis=2, tiled=True)  48.1 us
    all_to_all x2, waiting for transfers between devices, grid_transform(): lax.all_to_all(second, 'rows', split_axis=2, concat_axis=1, tiled=True)  45.5 us
    dot_general x14, matrix products, apply_small(): return jnp.einsum('rmk,mj->rjk', block, table, precision=highest)  44.6 us
    psum x1, blocking collectives, shards(): lax.psum((partial_coef, partial_loss), ('rows', 'cols'))  38 us
  transfers between devices with their start and end apart: 3, of which 3 were waited for; matrix products, arithmetic and copies ran while one was open for 3% of the time, Pallas kernels for 0%

commit v1 on v0

--- a/solution.py
+++ b/solution.py
@@ -7,6 +7,22 @@
 NG = 4096
 lasso_weight = 0.02
 ridge_weight = 0.1
+
+
+def exchange_in_pairs(shard, axis, split, join):
+    ways, here = (lax.axis_size(axis), lax.axis_index(axis))
+    width = shard.shape[split] // ways
+    lengths = list(shard.shape)
+    lengths[split] = width
+    height = lengths[join]
+    lengths[join] = height * ways
+    full = jnp.zeros(lengths, shard.dtype)
+    for mask in range(ways):
+        part = lax.dynamic_slice_in_dim(shard, (here ^ mask) * width, width, axis=split)
+        if mask:
+            part = lax.ppermute(part, axis, [(d, d ^ mask) for d in range(ways)])
+        full = lax.dynamic_update_slice_in_dim(full, part, (here ^ mask) * height, axis=join)
+    return full
 
 
 def field_spectrum(field_hyper, wave_row, wave_col):
@@ -73,7 +89,7 @@
     halfway = inverse_transform(full_rows, False)
     columns = middle_step(halfway)
     second = inverse_transform(columns, want_real)
-    blocks_out = lax.all_to_all(second, "rows", split_axis=2, concat_axis=1, tiled=True)
+    blocks_out = exchange_in_pairs(second, "rows", 2, 1)
     return jnp.swapaxes(blocks_out, 1, 2) * (1.0 / NG)
 
 

time: 906 us -> 935 us (1.032)
  waiting for transfers between devices: 139 us -> 197 us
  blocking collectives: 384 us -> 333 us
  matrix products: 198 us -> 216 us
  other arithmetic: 51.1 us -> 38.9 us
    all_to_all x2 -> x1, blocking collectives: 108 us -> 52.8 us  [middle_step(): lax.all_to_all(flipped, 'rows', split_axis=1, concat_axis=2, tiled=True)]
    ppermute x0 -> x14, waiting for transfers between devices: none -> 54.4 us  [exchange_in_pairs(): part = lax.ppermute(part, axis, [(d, d ^ mask) for d in range(ways)])]
    dot_general x14, matrix products: 44.6 us -> 57.2 us  [apply_small(): return jnp.einsum('rmk,mj->rjk', block, table, precision=highest)]
    ppermute x0 -> x14, starting transfers between devices: none -> 10.6 us  [exchange_in_pairs(): part = lax.ppermute(part, axis, [(d, d ^ mask) for d in range(ways)])]
    mul x2 -> x0, local copies, waits for them, and re-layouts: 9.44 us -> none  [grid_transform(): return jnp.swapaxes(blocks_out, 1, 2) * (1.0 / NG)]
    all_to_all x2 -> x1, waiting for transfers between devices: 45.5 us -> 49.1 us  [middle_step(): lax.all_to_all(flipped, 'rows', split_axis=1, concat_axis=2, tiled=True)]
  transfers between devices with their start and end apart: 3 -> 16, of which waited for: 3 -> 7; matrix products, arithmetic and copies ran while one was open for 3% -> 4% of each run, Pallas kernels for 0% -> 0%
where the time goes in v1:
time: 935 us; the launch traced here: 926 us
  blocking collectives  333 us (36%)
  matrix products  216 us (23%)
  waiting for transfers between devices  197 us (21%)
  local copies, waits for them, and re-layouts  110 us (12%)
  other arithmetic  38.9 us (4%)
  starting transfers between devices  21.8 us (2%)
    all_to_all x2, blocking collectives, middle_step(): lax.all_to_all(spread, 'cols', split_axis=2, concat_axis=1, tiled=True)  191 us
    dot_general x14, matrix products, apply_big(): return jnp.einsum('rnm,nk->rmk', block, table, precision=highest)  136 us
    all_to_all x1, waiting for transfers between devices, grid_transform(): lax.all_to_all(pieces, 'cols', split_axis=1, concat_axis=2, tiled=True)  93.3 us
    dot_general x14, matrix products, apply_small(): return jnp.einsum('rmk,mj->rjk', block, table, precision=highest)  57.2 us
    ppermute x14, waiting for transfers between devices, exchange_in_pairs(): part = lax.ppermute(part, axis, [(d, d ^ mask) for d in range(ways)])  54.4 us
    all_to_all x1, blocking collectives, middle_step(): lax.all_to_all(flipped, 'rows', split_axis=1, concat_axis=2, tiled=True)  52.8 us
    all_to_all x1, blocking collectives, grid_transform(): lax.all_to_all(pieces, 'cols', split_axis=1, concat_axis=2, tiled=True)  51.6 us
    all_to_all x1, waiting for transfers between devices, middle_step(): lax.all_to_all(flipped, 'rows', split_axis=1, concat_axis=2, tiled=True)  49.1 us
  transfers between devices with their start and end apart: 16, of which 7 were waited for; matrix products, arithmetic and copies ran while one was open for 4% of the time, Pallas kernels for 0%

profile of v1, /device:TPU:0, one launch (start us, length us, event | category | flops | bytes accessed | tf_op | source)
XLA Modules:
  0.0 925.9 jit_solution(12818683819105829969)
XLA Ops:
  4.6 3.8 multiply_bitcast_fusion.1
  12.1 5.8 pad_maximum_fusion
  17.9 6.5 all-to-all-start
  24.5 93.3 %all-to-all-done = f32[2,512,1024]{2,0,1:T(2,128)} async-done(((f32[2,512,1024]{2,0,1:T(2,128)}), f32[2,512,1024]{2,0,1:T(2,128)}, u32[]{:S(2)}, u32[]{:S(2)}) %all-to-all-start) | async-done | bytes 4194336 | tf_op jit(solution)/shard_map/all_to_all | solution.py:88
  127.4 10.3 %fusion.73 = f32[128,8,512]{2,0,1:T(8,128)} fusion(f32[128,512,8]{1,0,2:T(8,128)} %copy.180), kind=kOutput, calls=%fused_computation.113 | convolution fusion | flops 3224895488 | bytes 4194304 | tf_op jit(solution)/shard_map/rnm,nk->rmk/dot_general | solution.py:54
  137.7 8.4 fusion.61
  149.9 10.7 %convolution_subtract_fusion.2 = f32[128,8,512]{2,0,1:T(8,128)S(1)} fusion(f32[128,8,512]{2,0,1:T(8,128)} %fusion.73, f32[128,512,8]{1,0,2:T(8,128)S(1)} %copy.182), kind=kOutput, calls=%fused_computation.86 | convolution fusion | flops 3225419776 | bytes 6291456 | tf_op jit(solution)/shard_map/rnm,nk->rmk/dot_general | solution.py:54
  160.6 10.6 %multiply_subtract_fusion.3 = (f32[128,8,512]{2,0,1:T(8,128)S(1)}, f32[128,8,512]{2,0,1:T(8,128)S(1)}) fusion(f32[128,8,512]{2,0,1:T(8,128)S(1)} %convolution_subtract_fusion.2, f32[8,512]{1,0:T(8,128)S(1)} %get-tuple-element.48, f32[8,512]{1,0:T(8,128)S(1)} %get-tuple-element.49, f32[128,8,512]{2,0,1:T(8,128)S(1)} %copy-done.16, f32[128,512,8]{1,0,2:T(8,128)} %copy-done.1), kind=kOutput, calls=%fused_computation.54 | convolution fusion | flops 3228565504 | bytes 10518528 | tf_op jit(solution)/shard_map/rnm,nk->rmk/dot_general | solution.py:54
  174.1 4.2 fusion.30
  178.3 4.3 add_bitcast_fusion.2
  186.0 5.8 subtract_bitcast_fusion.3
  194.9 5.0 pad_maximum_fusion.1
  199.8 95.3 %all_to_all.96 = f32[2,128,4096]{1,0,2:T(2,128)S(1)} all-to-all(f32[2,128,4096]{1,0,2:T(2,128)S(1)} %pad_maximum_fusion.1), channel_id=1, replica_groups=mesh['rows'=8,'cols'=4] {'cols'}, dimensions={2} | all-to-all | bytes 8388608 | tf_op jit(solution)/shard_map/all_to_all | solution.py:82
  297.5 5.4 copy.192
  302.9 7.2 copy.193
  310.1 4.7 all-to-all-start.2
  314.9 49.1 %all-to-all-done.2 = f32[2,1024,512]{2,0,1:T(2,128)} async-done(((f32[2,1024,512]{2,0,1:T(2,128)}), f32[2,1024,512]{2,0,1:T(2,128)}, u32[]{:S(2)}, u32[]{:S(2)}) %all-to-all-start.2) | async-done | bytes 4194336 | tf_op jit(solution)/shard_map/all_to_all | solution.py:84
  373.4 10.3 %fusion.70 = f32[128,8,512]{2,0,1:T(8,128)} fusion(f32[128,512,8]{1,0,2:T(8,128)} %copy.196), kind=kOutput, calls=%fused_computation.110 | convolution fusion | flops 3224895488 | bytes 4194304 | tf_op jit(solution)/shard_map/rnm,nk->rmk/dot_general | solution.py:54
  383.7 8.4 fusion.58
  395.9 9.9 %convolution_subtract_fusion.1 = f32[128,8,512]{2,0,1:T(8,128)S(1)} fusion(f32[128,8,512]{2,0,1:T(8,128)} %fusion.70, f32[128,512,8]{1,0,2:T(8,128)S(1)} %copy.198), kind=kOutput, calls=%fused_computation.84 | convolution fusion | flops 3225419776 | bytes 6291456 | tf_op jit(solution)/shard_map/rnm,nk->rmk/dot_general | solution.py:54
  405.8 9.0 multiply_subtract_fusion.2
  426.9 23.3 %fusion = f32[1,512,1024]{2,0,1:T(1,128)} fusion(bf16[16,512,1024]{2,1,0:T(8,128)(2,1)} %param.9, f32[16]{0:T(128)S(1)} %copy-done.26), kind=kOutput, calls=%fused_computation.1 | convolution fusion | flops 100663296 | bytes 18874432 | tf_op jit(solution)/shard_map/j,jrc->rc/dot_general | solution.py:108
  457.7 12.9 %collective-permute-done.3 = f32[1,128,512]{1,2,0:T(8,128)S(1)} collective-permute-done((f32[1,128,512]{1,2,0:T(8,128)S(1)}, f32[1,128,512]{1,2,0:T(8,128)S(1)}, u32[]{:S(2)}, u32[]{:S(2)}) %collective-permute-start.3) | collective-permute-done | bytes 262176 | tf_op jit(solution)/shard_map/ppermute | solution.py:23
  470.7 4.3 collective-permute-done.4
  475.1 3.9 multiply_reduce_fusion.1
  480.5 51.6 %all_to_all.97 = f32[1,512,1024]{2,0,1:T(1,128)S(1)} all-to-all(f32[1,512,1024]{2,0,1:T(1,128)S(1)} %broadcast_in_dim.8), channel_id=1, replica_groups=mesh['rows'=8,'cols'=4] {'cols'}, dimensions={1} | all-to-all | bytes 4194304 | tf_op jit(solution)/shard_map/all_to_all | solution.py:88
  537.6 8.4 fusion.67
  546.0 10.5 %multiply_subtract_fusion.1 = (f32[128,8,512]{2,0,1:T(8,128)S(1)}, f32[128,8,512]{2,0,1:T(8,128)S(1)}) fusion(f32[128,8,512]{2,0,1:T(8,128)S(1)} %fusion.67, f32[8,512]{1,0:T(8,128)S(1)} %get-tuple-element.48, f32[8,512]{1,0:T(8,128)S(1)} %get-tuple-element.49, f32[128,512,8]{1,0,2:T(8,128)} %copy-done.18), kind=kOutput, calls=%fused_computation.46 | convolution fusion | flops 3228041216 | bytes 8421376 | tf_op jit(solution)/shard_map/rnm,nk->rmk/dot_general | solution.py:54
  559.3 4.2 fusion.22
  563.6 4.3 add_bitcast_fusion.1
  570.8 5.8 subtract_bitcast_fusion.1
  579.7 5.0 pad_maximum_fusion.2
  584.7 95.7 %all_to_all.98 = f32[2,128,4096]{1,0,2:T(2,128)S(1)} all-to-all(f32[2,128,4096]{1,0,2:T(2,128)S(1)} %pad_maximum_fusion.2), channel_id=1, replica_groups=mesh['rows'=8,'cols'=4] {'cols'}, dimensions={2} | all-to-all | bytes 8388608 | tf_op jit(solution)/shard_map/all_to_all | solution.py:82
  682.6 5.4 copy.221
  688.0 7.2 copy.222
  695.2 52.8 %all_to_all.99 = f32[2,1024,512]{2,0,1:T(2,128)S(1)} all-to-all(f32[2,1024,512]{2,0,1:T(2,128)} %copy.222), channel_id=1, replica_groups=mesh['rows'=8,'cols'=4] {'rows'}, dimensions={1} | all-to-all | bytes 8388608 | tf_op jit(solution)/shard_map/all_to_all | solution.py:84
  755.4 10.3 %fusion.65 = f32[128,8,512]{2,0,1:T(8,128)} fusion(f32[128,512,8]{1,0,2:T(8,128)} %copy.225), kind=kOutput, calls=%fused_computation.105 | convolution fusion | flops 3224895488 | bytes 4194304 | tf_op jit(solution)/shard_map/rnm,nk->rmk/dot_general | solution.py:54
  765.6 8.4 fusion.53
  779.1 9.9 %convolution_subtract_fusion = f32[128,8,512]{2,0,1:T(8,128)S(1)} fusion(f32[128,8,512]{2,0,1:T(8,128)} %fusion.65, f32[128,512,8]{1,0,2:T(8,128)S(1)} %copy.227), kind=kOutput, calls=%fused_computation.82 | convolution fusion | flops 3225419776 | bytes 6291456 | tf_op jit(solution)/shard_map/rnm,nk->rmk/dot_general | solution.py:54
  789.0 10.7 %multiply_subtract_fusion = (f32[128,8,512]{2,0,1:T(8,128)S(1)}, f32[128,8,512]{2,0,1:T(8,128)S(1)}) fusion(f32[128,8,512]{2,0,1:T(8,128)S(1)} %convolution_subtract_fusion, f32[8,512]{1,0:T(8,128)S(1)} %get-tuple-element.48, f32[8,512]{1,0:T(8,128)S(1)} %get-tuple-element.49, f32[128,8,512]{2,0,1:T(8,128)S(1)} %copy-done.15, f32[128,512,8]{1,0,2:T(8,128)} %copy-done), kind=kOutput, calls=%fused_computation.42 | convolution fusion | flops 3228565504 | bytes 10518528 | tf_op jit(solution)/shard_map/rnm,nk->rmk/dot_general | solution.py:54
  802.7 4.2 fusion.12
  806.9 4.2 subtract_bitcast_fusion
  814.2 5.8 add_bitcast_fusion
  829.8 7.5 multiply_reduce_fusion
  841.1 10.3 %collective-permute-done.9 = f32[2,128,512]{1,2,0:T(8,128)S(1)} collective-permute-done((f32[2,128,512]{1,2,0:T(8,128)S(1)}, f32[2,128,512]{1,2,0:T(8,128)S(1)}, u32[]{:S(2)}, u32[]{:S(2)}) %collective-permute-start.9) | collective-permute-done | bytes 524320 | tf_op jit(solution)/shard_map/ppermute | solution.py:23
  851.5 23.9 %collective-permute-done.11 = f32[2,128,512]{1,2,0:T(8,128)S(1)} collective-permute-done((f32[2,128,512]{1,2,0:T(8,128)S(1)}, f32[2,128,512]{1,2,0:T(8,128)S(1)}, u32[]{:S(2)}, u32[]{:S(2)}) %collective-permute-start.11) | collective-permute-done | bytes 524320 | tf_op jit(solution)/shard_map/ppermute | solution.py:23
  877.9 4.3 fusion.4
  883.4 38.0 %all-reduce = (f32[16]{0:T(128)S(1)}, f32[]{:T(128)}) all-reduce(f32[16]{0:T(128)S(1)} %multiply_reduce_fusion, f32[]{:T(128)S(6)} %add.345), channel_id=1, replica_groups=mesh['rows'=8,'cols'=4] {'rows','cols'}, use_global_device_ids=true, to_apply=%region_0.1 | all-reduce | flops 17 | bytes 136 | tf_op jit(solution)/shard_map/psum | solution.py:119
  (141 shorter events, 116.6 us)
Async XLA Ops:
  3.3 5.2 copy-start.22
  3.3 5.2 copy-start.24
  17.9 99.9 %all-to-all-start = ((f32[2,512,1024]{2,0,1:T(2,128)}), f32[2,512,1024]{2,0,1:T(2,128)}, u32[]{:S(2)}, u32[]{:S(2)}) async-start(f32[2,512,1024]{2,0,1:T(2,128)} %pad_maximum_fusion), calls=%async_computation | async-start | bytes 8388608 | tf_op jit(solution)/shard_map/all_to_all | solution.py:88
  127.4 10.3 %copy-start.19 = (f32[128,512,8]{1,0,2:T(8,128)S(1)}, f32[128,512,8]{1,0,2:T(8,128)}, u32[]{:S(2)}) copy-start(f32[128,512,8]{1,0,2:T(8,128)} %copy.180) | copy-start | bytes 6291460
  137.7 8.4 copy-start.9
  149.8 10.7 %copy-start.1 = (f32[128,512,8]{1,0,2:T(8,128)}, f32[128,512,8]{1,0,2:T(8,128)S(1)}, u32[]{:S(2)}) copy-start(f32[128,512,8]{1,0,2:T(8,128)S(1)} %copy.182) | copy-start | bytes 6291460
  149.9 10.7 %copy-start.16 = (f32[128,8,512]{2,0,1:T(8,128)S(1)}, f32[128,8,512]{2,0,1:T(8,128)}, u32[]{:S(2)}) copy-start(f32[128,8,512]{2,0,1:T(8,128)} %fusion.61) | copy-start | bytes 6291460
  191.7 3.1 copy-start.12
  310.1 53.9 %all-to-all-start.2 = ((f32[2,1024,512]{2,0,1:T(2,128)}), f32[2,1024,512]{2,0,1:T(2,128)}, u32[]{:S(2)}, u32[]{:S(2)}) async-start(f32[2,1024,512]{2,0,1:T(2,128)} %copy.193), calls=%async_computation.2 | async-start | bytes 8388608 | tf_op jit(solution)/shard_map/all_to_all | solution.py:84
  373.4 10.3 %copy-start.20 = (f32[128,512,8]{1,0,2:T(8,128)S(1)}, f32[128,512,8]{1,0,2:T(8,128)}, u32[]{:S(2)}) copy-start(f32[128,512,8]{1,0,2:T(8,128)} %copy.196) | copy-start | bytes 6291460
  383.7 8.4 copy-start.10
  395.9 10.0 %copy-start.17 = (f32[128,8,512]{2,0,1:T(8,128)S(1)}, f32[128,8,512]{2,0,1:T(8,128)}, u32[]{:S(2)}) copy-start(f32[128,8,512]{2,0,1:T(8,128)} %fusion.58) | copy-start | bytes 6291460
  422.5 1.6 copy-start.6
  424.1 2.8 copy-start.26
  425.0 26.9 %collective-permute-start = (f32[1,128,512]{1,2,0:T(8,128)}, f32[1,128,512]{1,2,0:T(8,128)}, u32[]{:S(2)}, u32[]{:S(2)}) collective-permute-start(f32[1,128,512]{1,2,0:T(8,128)} %get-tuple-element.41), channel_id=1, source_target_pairs={{0,4},{4,0},{8,12},{12,8},{16,20},{20,16},{24,28},{28,24},{1,5},{5... | collective-permute-start | bytes 786440 | tf_op jit(solution)/shard_map/ppermute | solution.py:23
  425.0 28.4 %collective-permute-start.1 = (f32[1,128,512]{1,2,0:T(8,128)}, f32[1,128,512]{1,2,0:T(8,128)}, u32[]{:S(2)}, u32[]{:S(2)}) collective-permute-start(f32[1,128,512]{1,2,0:T(8,128)} %get-tuple-element.40), channel_id=1, source_target_pairs={{0,8},{4,12},{8,0},{12,4},{16,24},{20,28},{24,16},{28,20},{1,9},{5... | collective-permute-start | bytes 786440 | tf_op jit(solution)/shard_map/ppermute | solution.py:23
  425.6 31.1 %collective-permute-start.2 = (f32[1,128,512]{1,2,0:T(8,128)S(1)}, f32[1,128,512]{1,2,0:T(8,128)}, u32[]{:S(2)}, u32[]{:S(2)}) collective-permute-start(f32[1,128,512]{1,2,0:T(8,128)S(1)} %get-tuple-element.39), channel_id=1, source_target_pairs={{0,12},{4,8},{8,4},{12,0},{16,28},{20,24},{24,20},{28,16},{1,13},{... | collective-permute-start | bytes 786440 | tf_op jit(solution)/shard_map/ppermute | solution.py:23
  450.2 24.9 %copy-start.14 = (f32[1,512,1024]{2,0,1:T(1,128)S(1)}, f32[1,512,1024]{2,0,1:T(1,128)}, u32[]{:S(2)}) copy-start(f32[1,512,1024]{2,0,1:T(1,128)} %fusion) | copy-start | bytes 6291460
  450.2 20.4 %collective-permute-start.3 = (f32[1,128,512]{1,2,0:T(8,128)S(1)}, f32[1,128,512]{1,2,0:T(8,128)S(1)}, u32[]{:S(2)}, u32[]{:S(2)}) collective-permute-start(f32[1,128,512]{1,2,0:T(8,128)S(1)} %get-tuple-element.38), channel_id=1, source_target_pairs={{0,16},{4,20},{8,24},{12,28},{16,0},{20,4},{24,8},{28,12},{1,17},{... | collective-permute-start | bytes 786440 | tf_op jit(solution)/shard_map/ppermute | solution.py:23
  450.8 24.2 %collective-permute-start.4 = (f32[1,128,512]{1,2,0:T(8,128)S(1)}, f32[1,128,512]{1,2,0:T(8,128)S(1)}, u32[]{:S(2)}, u32[]{:S(2)}) collective-permute-start(f32[1,128,512]{1,2,0:T(8,128)S(1)} %get-tuple-element.37), channel_id=1, source_target_pairs={{0,20},{4,16},{8,28},{12,24},{16,4},{20,0},{24,12},{28,8},{1,21},{... | collective-permute-start | bytes 786440 | tf_op jit(solution)/shard_map/ppermute | solution.py:23
  451.9 23.1 %collective-permute-start.5 = (f32[1,128,512]{1,2,0:T(8,128)S(1)}, f32[1,128,512]{1,2,0:T(8,128)S(1)}, u32[]{:S(2)}, u32[]{:S(2)}) collective-permute-start(f32[1,128,512]{1,2,0:T(8,128)S(1)} %get-tuple-element.36), channel_id=1, source_target_pairs={{0,24},{4,28},{8,16},{12,20},{16,8},{20,12},{24,0},{28,4},{1,25},{... | collective-permute-start | bytes 786440 | tf_op jit(solution)/shard_map/ppermute | solution.py:23
  453.5 21.6 %collective-permute-start.6 = (f32[1,128,512]{1,2,0:T(8,128)S(1)}, f32[1,128,512]{1,2,0:T(8,128)S(1)}, u32[]{:S(2)}, u32[]{:S(2)}) collective-permute-start(f32[1,128,512]{1,2,0:T(8,128)S(1)} %get-tuple-element.35), channel_id=1, source_target_pairs={{0,28},{4,24},{8,20},{12,16},{16,12},{20,8},{24,4},{28,0},{1,29},{... | collective-permute-start | bytes 786440 | tf_op jit(solution)/shard_map/ppermute | solution.py:23
  479.0 1.4 copy-start.4
  536.3 1.3 copy-start.18
  576.5 3.1 copy-start.13
  755.4 10.3 %copy-start.21 = (f32[128,512,8]{1,0,2:T(8,128)S(1)}, f32[128,512,8]{1,0,2:T(8,128)}, u32[]{:S(2)}) copy-start(f32[128,512,8]{1,0,2:T(8,128)} %copy.225) | copy-start | bytes 6291460
  765.6 8.4 copy-start.11
  777.8 1.3 copy-start
  779.1 9.9 %copy-start.15 = (f32[128,8,512]{2,0,1:T(8,128)S(1)}, f32[128,8,512]{2,0,1:T(8,128)}, u32[]{:S(2)}) copy-start(f32[128,8,512]{2,0,1:T(8,128)} %fusion.53) | copy-start | bytes 6291460
  820.0 3.1 copy-start.2
  824.4 1.6 copy-start.3
  825.9 3.9 copy-start.5
  826.2 11.2 %collective-permute-start.7 = (f32[2,128,512]{1,2,0:T(8,128)S(1)}, f32[2,128,512]{1,2,0:T(8,128)S(1)}, u32[]{:S(2)}, u32[]{:S(2)}) collective-permute-start(f32[2,128,512]{1,2,0:T(8,128)S(1)} %get-tuple-element.23), channel_id=1, source_target_pairs={{0,4},{4,0},{8,12},{12,8},{16,20},{20,16},{24,28},{28,24},{1,5},{5... | collective-permute-start | bytes 1572872 | tf_op jit(solution)/shard_map/ppermute | solution.py:23
  826.2 14.8 %collective-permute-start.8 = (f32[2,128,512]{1,2,0:T(8,128)S(1)}, f32[2,128,512]{1,2,0:T(8,128)S(1)}, u32[]{:S(2)}, u32[]{:S(2)}) collective-permute-start(f32[2,128,512]{1,2,0:T(8,128)S(1)} %get-tuple-element.24), channel_id=1, source_target_pairs={{0,8},{4,12},{8,0},{12,4},{16,24},{20,28},{24,16},{28,20},{1,9},{5... | collective-permute-start | bytes 1572872 | tf_op jit(solution)/shard_map/ppermute | solution.py:23
  826.9 24.5 %collective-permute-start.9 = (f32[2,128,512]{1,2,0:T(8,128)S(1)}, f32[2,128,512]{1,2,0:T(8,128)S(1)}, u32[]{:S(2)}, u32[]{:S(2)}) collective-permute-start(f32[2,128,512]{1,2,0:T(8,128)S(1)} %get-tuple-element.25), channel_id=1, source_target_pairs={{0,12},{4,8},{8,4},{12,0},{16,28},{20,24},{24,20},{28,16},{1,13},{... | collective-permute-start | bytes 1572872 | tf_op jit(solution)/shard_map/ppermute | solution.py:23
  828.1 23.3 %collective-permute-start.10 = (f32[2,128,512]{1,2,0:T(8,128)S(1)}, f32[2,128,512]{1,2,0:T(8,128)S(1)}, u32[]{:S(2)}, u32[]{:S(2)}) collective-permute-start(f32[2,128,512]{1,2,0:T(8,128)S(1)} %get-tuple-element.27), channel_id=1, source_target_pairs={{0,16},{4,20},{8,24},{12,28},{16,0},{20,4},{24,8},{28,12},{1,17},{... | collective-permute-start | bytes 1572872 | tf_op jit(solution)/shard_map/ppermute | solution.py:23
  828.7 46.8 %collective-permute-start.11 = (f32[2,128,512]{1,2,0:T(8,128)S(1)}, f32[2,128,512]{1,2,0:T(8,128)S(1)}, u32[]{:S(2)}, u32[]{:S(2)}) collective-permute-start(f32[2,128,512]{1,2,0:T(8,128)S(1)} %get-tuple-element.28), channel_id=1, source_target_pairs={{0,20},{4,16},{8,28},{12,24},{16,4},{20,0},{24,12},{28,8},{1,21},{... | collective-permute-start | bytes 1572872 | tf_op jit(solution)/shard_map/ppermute | solution.py:23
  837.4 38.1 %collective-permute-start.12 = (f32[2,128,512]{1,2,0:T(8,128)S(1)}, f32[2,128,512]{1,2,0:T(8,128)S(1)}, u32[]{:S(2)}, u32[]{:S(2)}) collective-permute-start(f32[2,128,512]{1,2,0:T(8,128)S(1)} %get-tuple-element.26), channel_id=1, source_target_pairs={{0,24},{4,28},{8,16},{12,20},{16,8},{20,12},{24,0},{28,4},{1,25},{... | collective-permute-start | bytes 1572872 | tf_op jit(solution)/shard_map/ppermute | solution.py:23
  841.0 34.5 %collective-permute-start.13 = (f32[2,128,512]{1,2,0:T(8,128)S(1)}, f32[2,128,512]{1,2,0:T(8,128)S(1)}, u32[]{:S(2)}, u32[]{:S(2)}) collective-permute-start(f32[2,128,512]{1,2,0:T(8,128)S(1)} %get-tuple-element.21), channel_id=1, source_target_pairs={{0,28},{4,24},{8,20},{12,16},{16,12},{20,8},{24,4},{28,0},{1,29},{... | collective-permute-start | bytes 1572872 | tf_op jit(solution)/shard_map/ppermute | solution.py:23
  875.7 1.6 copy-start.7
  875.7 2.2 copy-start.8
  875.7 2.2 copy-start.23
  875.7 2.2 copy-start.25
